TPU v7x, 512 devices: a whole 4x4x16 slice. The times are simulated.
512 devices in a mesh: grp: 16 (over z), tp: 32 (over y, x, core).
Axes of the slice: x: 4, y: 4, z: 16, core: 2. Of those that a mesh axis runs over, the one named last changes fastest.
Arguments:
- attention_output: bfloat16 [512, 8192], P('grp', 'tp'), may hold values from -6 to 6
- output_projection: bfloat16 [8192, 8192], P('tp', 'grp'), may hold values from -0.0625 to 0.0625
- adapter_down_weight: bfloat16 [256, 8192, 64], P('grp', 'tp'), may hold values from -0.0625 to 0.0625
- adapter_up_weight: bfloat16 [256, 64, 8192], P('tp', None, 'grp'), may hold values from -0.75 to 0.75
- residual: bfloat16 [512, 8192], P('tp', 'grp')
- final_norm_gain: bfloat16 [8192], P('grp'), may hold values from 0.5 to 1.5
- vocab_head_weight: bfloat16 [8192, 65536], P('grp', 'tp')
- row_adapter_index: int32 [512], replicated, may hold values from 0 to 255, as said below
- row_grammar_state: int32 [512], replicated, may hold values from 0 to 39
- grammar_token_bits: int32 [40, 2048], P(None, 'tp'), may hold values from -2147483647 to 2147483647, as said below
Outputs:
- log_probs: float32 [512, 65536], P('grp', 'tp')
Inputs may be any that keep to these rules, and one draw needn't show every extreme that they name: `row_adapter_index`: no adapter is named by more than 4 rows; at least one is named by exactly 4. `grammar_token_bits`: the lowest bit of every word is set.
All inputs are finite; a program needn't handle non-finite values.
Results may differ from a plain program's by a relative error of at most 0.00105.
The roundings to bfloat16 on the way count: a program that leaves them out, or rounds other values in their place, can miss the bound.
Values may be sent and summed in bfloat16 or wider, within the bound.
No kernel may reach another device: no remote copies, remote signals or barrier semaphores. Data moves between devices by JAX's collectives and lax.ppermute only.
A program may use at most 64 MiB of HBM per device.

v0:
```python
import jax
import jax.numpy as jnp
from jax import lax
from jax.sharding import PartitionSpec as P

MODEL_WIDTH = 8192
MOST = 4


EPSILON = 1e-05


def combined_all(value, axis, join):
    pieces = jax.tree.map(lambda part: lax.all_gather(part, axis), value)
    head = jax.tree.map(lambda part: part[0], pieces)
    tail = jax.tree.map(lambda part: part[1:], pieces)
    running, _ = lax.scan(lambda running, share: (join(running, share), None), head, tail)
    return running


def slot_table(row_adapter_index, adapter_count):
    numbers = jnp.arange(adapter_count, dtype=jnp.int32)
    matches = (row_adapter_index[None, :] == numbers[:, None]).astype(jnp.int32)
    places = jnp.cumsum(matches, axis=1) - 1
    heat_tiers = jnp.arange(MOST, dtype=jnp.int32)
    return (matches[:, None, :] == 1) & (places[:, None, :] == heat_tiers[None, :, None])


def unpack_bits(packed):
    shifts = jnp.arange(32, dtype=jnp.int32)
    bits_out = jnp.bitwise_and(jnp.right_shift(packed[:, :, None], shifts[None, None, :]), 1)
    return bits_out.reshape(packed.shape[0], packed.shape[1] * 32).astype(jnp.float32)


def row_masks(mask_table, states):
    onehot_rows = (
        states[:, None] == jnp.arange(mask_table.shape[0], dtype=jnp.int32)[None, :]
    ).astype(jnp.float32)
    return jnp.dot(onehot_rows, mask_table, precision=lax.Precision.HIGHEST) > 0.5


def softmax_parts(logits, allowed):
    masked = jnp.where(allowed, logits, -jnp.inf)
    highest = jnp.max(masked, axis=1)
    summed = jnp.sum(jnp.exp(masked - highest[:, None]), axis=1)
    return (highest, summed)


def combine_stats(first_stats, second_stats):
    highest = jnp.maximum(first_stats[0], second_stats[0])
    summed = first_stats[1] * jnp.exp(first_stats[0] - highest) + second_stats[1] * jnp.exp(
        second_stats[0] - highest
    )
    return (highest, summed)


def body(
    attention_output,
    output_projection,
    adapter_down_weight,
    adapter_up_weight,
    residual,
    final_norm_gain,
    vocab_head_weight,
    row_adapter_index,
    row_grammar_state,
    grammar_token_bits,
):
    grp_index = lax.axis_index("grp")
    tp_index = lax.axis_index("tp")
    all_rows = lax.all_gather(attention_output, "grp", axis=0, tiled=True)
    per_group = adapter_down_weight.shape[0]
    per_tensor_part = adapter_up_weight.shape[0]
    adapter_count = per_tensor_part * lax.axis_size("tp")
    slot_mask = slot_table(row_adapter_index, adapter_count)
    down_select = lax.dynamic_slice_in_dim(slot_mask, grp_index * per_group, per_group, 0).astype(
        jnp.bfloat16
    )
    slot_row_list = jnp.einsum(
        "amr,rf->amf", down_select, all_rows, preferred_element_type=jnp.float32
    ).astype(jnp.bfloat16)
    partial_latent = jnp.einsum(
        "cse,ceu->csu", slot_row_list, adapter_down_weight, preferred_element_type=jnp.float32
    )
    padded = jnp.zeros((adapter_count,) + partial_latent.shape[1:], jnp.float32)
    padded = lax.dynamic_update_slice_in_dim(padded, partial_latent, grp_index * per_group, 0)
    latent_all = lax.psum(padded, ("grp", "tp")).astype(jnp.bfloat16)
    local_latent = lax.dynamic_slice_in_dim(
        latent_all, tp_index * per_tensor_part, per_tensor_part, 0
    )
    slot_delta = jnp.einsum(
        "tsl,tlx->tsx", local_latent, adapter_up_weight, preferred_element_type=jnp.float32
    )
    up_select = lax.dynamic_slice_in_dim(
        slot_mask, tp_index * per_tensor_part, per_tensor_part, 0
    ).astype(jnp.float32)
    delta_rows = jnp.einsum("amr,amf->rf", up_select, slot_delta, precision=lax.Precision.HIGHEST)
    term_sum = jnp.dot(all_rows, output_projection, preferred_element_type=jnp.float32) + delta_rows
    own_rows = residual.shape[0]
    term_sum = term_sum + lax.dynamic_update_slice_in_dim(
        jnp.zeros_like(term_sum), residual.astype(jnp.float32), tp_index * own_rows, 0
    )
    layer_out = lax.psum(term_sum, "tp").astype(jnp.bfloat16)
    layer_float = layer_out.astype(jnp.float32)
    square_part = jnp.sum(layer_float * layer_float, axis=1)
    scaled = (layer_float * final_norm_gain.astype(jnp.float32)[None, :]).astype(jnp.bfloat16)
    logit_part = jnp.dot(scaled, vocab_head_weight, preferred_element_type=jnp.float32)
    logit_rows, squares = (
        lax.psum_scatter(logit_part, "grp", scatter_dimension=0, tiled=True),
        lax.psum_scatter(square_part, "grp", scatter_dimension=0, tiled=True),
    )
    factor = lax.rsqrt(squares / MODEL_WIDTH + EPSILON)
    logits = logit_rows * factor[:, None]
    own_count = logits.shape[0]
    states = lax.dynamic_slice_in_dim(row_grammar_state, grp_index * own_count, own_count, 0)
    allowed = row_masks(unpack_bits(grammar_token_bits), states)
    highest, summed = softmax_parts(logits, allowed)
    highest, summed = combined_all((highest, summed), "tp", combine_stats)
    return jnp.where(allowed, logits - highest[:, None] - jnp.log(summed)[:, None], 0.0)


def solution(mesh):
    in_specs = (
        P("grp", "tp"),
        P("tp", "grp"),
        P("grp", "tp", None),
        P("tp", None, "grp"),
        P("tp", "grp"),
        P("grp"),
        P("grp", "tp"),
        P(),
        P(),
        P(None, "tp"),
    )
    out_specs = P("grp", "tp")
    return jax.shard_map(body, mesh=mesh, in_specs=in_specs, out_specs=out_specs, check_vma=False)
```

profile of v0, /device:TPU:1, one launch (start us, length us, event | category | flops | bytes accessed | tf_op | source)
XLA Modules:
  0.0 449.1 jit_solution(10779886343093437935)
XLA Ops:
  6.5 0.9 convert_compare_fusion
  7.5 0.8 copy.14
  8.3 0.2 fusion.11
  8.7 0.2 copy.16
  9.0 30.6 %all_gather.15 = bf16[512,256]{1,0:T(8,128)(2,1)S(1)} all-gather(bf16[32,256]{1,0:T(8,128)(2,1)S(1)} %copy-done.5), channel_id=1, replica_groups=mesh['grp'=16,'tp'=32] {'grp'}, dimensions={0}, use_global_device_ids=true | all-gather | bytes 278528 | tf_op jit(solution)/shard_map/all_gather | solution.py:71
  39.6 0.4 fusion.5
  39.9 0.2 convolution_convert_fusion
  40.1 0.6 copy-done.2
  40.8 0.2 convolution_dynamic-update-slice_fusion
  41.1 110.8 %all-reduce.6 = bf16[256,4,64]{2,1,0:T(4,128)(2,1)S(1)} all-reduce(f32[256,4,64]{2,1,0:T(4,128)S(1)} %convolution_dynamic-update-slice_fusion), channel_id=1, replica_groups=mesh['grp'=16,'tp'=32] {'grp','tp'}, use_global_device_ids=true, to_apply=%region_2.3 | all-reduce | flops 65536 | bytes 393216 | tf_op jit(solution)/shard_map/psum | solution.py:87
  151.9 1.2 fusion.26
  153.1 1.4 convolution_bitcast_fusion
  154.5 2.2 convolution_add_fusion
  156.7 1.4 add_dynamic-update-slice_fusion
  158.1 132.8 %all-reduce.7 = bf16[512,512]{1,0:T(8,128)(2,1)S(1)} all-reduce(f32[512,512]{1,0:T(8,128)} %add_dynamic-update-slice_fusion), channel_id=1, replica_groups=mesh['grp'=16,'tp'=32] {'tp'}, use_global_device_ids=true, to_apply=%region_3.4 | all-reduce | flops 262144 | bytes 1572864 | tf_op jit(solution)/shard_map/psum | solution.py:103
  290.9 3.2 fusion.8
  294.2 0.7 copy-done.4
  294.9 0.4 shift_right_arithmetic.20
  295.3 1.3 shift_right_arithmetic.21
  296.7 1.3 dynamic-slice.3
  298.6 0.8 dynamic_slice.19
  299.3 1.3 dynamic-slice.1
  301.2 1.2 fusion.7
  302.5 23.1 %all-reduce.2 = f32[512]{0:T(512)S(1)} all-reduce(f32[512]{0:T(512)S(1)} %fusion.7), channel_id=5, replica_groups=mesh['grp'=16,'tp'=32] {'grp'}, use_global_device_ids=true, to_apply=%region_6.7.clone | all-reduce | flops 512 | bytes 4096
  325.7 36.9 %reduce-scatter.2.cloned.1.call-done = f32[32,2048]{1,0:T(8,128)} async-done(((f32[512,2048]{1,0:T(8,128)}), f32[32,2048]{1,0:T(8,128)}) %reduce-scatter.2.cloned.1.call-update) | async-done | bytes 262160 | tf_op jit(solution)/shard_map/reduce_scatter | solution.py:109
  362.5 1.5 fusion.19
  364.0 0.2 dynamic-update-slice.1
  364.3 1.2 exponential_reduce_fusion
  365.5 0.2 dynamic-update-slice.2
  365.7 73.1 %all-reduce.3 = (f32[1024]{0:T(1024)S(1)}, f32[1024]{0:T(1024)S(1)}) all-reduce(f32[1024]{0:T(1024)S(1)} %dynamic-update-slice.1, f32[1024]{0:T(1024)S(1)} %dynamic-update-slice.2), channel_id=2, replica_groups=mesh['grp'=16,'tp'=32] {'tp'}, use_global_device_ids=true, to_apply=%add | all-reduce | flops 2048 | bytes 16384
  439.2 1.3 while.12
  440.5 1.8 subtract_select_fusion
  (66 shorter events, 1.7 us)
Async XLA Ops:
  6.5 284.4 %copy-start = (bf16[512,2048]{1,0:T(8,128)(2,1)S(1)}, bf16[512,2048]{1,0:T(8,128)(2,1)}, u32[]{:S(2)}) copy-start(bf16[512,2048]{1,0:T(8,128)(2,1)} %param.18) | copy-start | bytes 6291460
  6.5 2.4 copy-start.5
  6.5 356.0 %reduce-scatter.2.cloned.1.call-start = ((), (), s32[]{:S(2)}) async-start(), calls=%async_computation.1 | async-start | bytes 4456448 | tf_op jit(solution)/shard_map/reduce_scatter | solution.py:109
  9.0 31.8 %copy-start.3 = (bf16[16,256,64]{1,2,0:T(8,128)(2,1)S(1)}, bf16[16,256,64]{1,2,0:T(8,128)(2,1)}, u32[]{:S(2)}) copy-start(bf16[16,256,64]{1,2,0:T(8,128)(2,1)} %param.14) | copy-start | bytes 1572868
  39.9 0.8 copy-start.2
  153.1 3.6 copy-start.6
  154.5 136.4 %copy-start.7 = (bf16[512]{0:T(512)(128)(2,1)S(1)}, bf16[512]{0:T(512)(128)(2,1)}, u32[]{:S(2)}) copy-start(bf16[512]{0:T(512)(128)(2,1)} %param.17) | copy-start | bytes 3076
  290.9 3.2 copy-start.1
  294.1 0.7 copy-start.4
Sparse Core Ops, SparseCore 0:
  294.3 68.1 reduce-scatter.1
where the time goes:
time: 450 us; the launch traced here: 449 us
  blocking collectives  370 us (82%)
  waiting for transfers between devices  36.9 us (8%)
  between operations  14.8 us (3%)
  matrix products  9.92 us (2%)
  local copies, waits for them, and re-layouts  8.44 us (2%)
  other arithmetic  8.17 us (2%)
    psum x1, blocking collectives, body(): layer_out = lax.psum(term_sum, 'tp').astype(jnp.bfloat16)  133 us
    psum x1, blocking collectives, body(): latent_all = lax.psum(padded, ('grp', 'tp')).astype(jnp.bfloat16)  111 us
    unnamed x2, blocking collectives  96.2 us
    reduce_scatter x1, waiting for transfers between devices, body(): lax.psum_scatter(logit_part, 'grp', scatter_dimension=0, tiled=True)  36.9 us
    all_gather x1, blocking collectives, body(): all_rows = lax.all_gather(attention_output, 'grp', axis=0, tiled=True)  30.6 us
  transfers between devices with their start and end apart: 1, of which 1 were waited for; matrix products, arithmetic and copies ran while one was open for 1% of the time, Pallas kernels for 0%

commit v1 on v0

--- a/solution.py
+++ b/solution.py
@@ -10,12 +10,18 @@
 EPSILON = 1e-05
 
 
-def combined_all(value, axis, join):
-    pieces = jax.tree.map(lambda part: lax.all_gather(part, axis), value)
-    head = jax.tree.map(lambda part: part[0], pieces)
-    tail = jax.tree.map(lambda part: part[1:], pieces)
-    running, _ = lax.scan(lambda running, share: (join(running, share), None), head, tail)
-    return running
+TP_Y = 4
+TP_XC = 8
+ACROSS_Y = [[TP_XC * y + k for y in range(TP_Y)] for k in range(TP_XC)]
+ACROSS_XC = [[TP_XC * y + k for k in range(TP_XC)] for y in range(TP_Y)]
+
+
+def exchange(blocks, axis, groups=None):
+    return lax.all_to_all(blocks, axis, 0, 0, tiled=True, axis_index_groups=groups)
+
+
+def gathered(value, axis, count, groups=None):
+    return exchange(jnp.broadcast_to(value[None], (count,) + value.shape), axis, groups)
 
 
 def slot_table(row_adapter_index, adapter_count):
@@ -46,14 +52,6 @@
     return (highest, summed)
 
 
-def combine_stats(first_stats, second_stats):
-    highest = jnp.maximum(first_stats[0], second_stats[0])
-    summed = first_stats[1] * jnp.exp(first_stats[0] - highest) + second_stats[1] * jnp.exp(
-        second_stats[0] - highest
-    )
-    return (highest, summed)
-
-
 def body(
     attention_output,
     output_projection,
@@ -68,10 +66,14 @@
 ):
     grp_index = lax.axis_index("grp")
     tp_index = lax.axis_index("tp")
-    all_rows = lax.all_gather(attention_output, "grp", axis=0, tiled=True)
+    grp_size, tp_size = lax.axis_size("grp"), lax.axis_size("tp")
+    features = attention_output.shape[1]
+    all_rows = gathered(attention_output, "grp", grp_size).reshape(-1, features)
+    row_total = all_rows.shape[0]
     per_group = adapter_down_weight.shape[0]
+    rank = adapter_down_weight.shape[2]
     per_tensor_part = adapter_up_weight.shape[0]
-    adapter_count = per_tensor_part * lax.axis_size("tp")
+    adapter_count = per_tensor_part * tp_size
     slot_mask = slot_table(row_adapter_index, adapter_count)
     down_select = lax.dynamic_slice_in_dim(slot_mask, grp_index * per_group, per_group, 0).astype(
         jnp.bfloat16
@@ -81,12 +83,14 @@
     ).astype(jnp.bfloat16)
     partial_latent = jnp.einsum(
         "cse,ceu->csu", slot_row_list, adapter_down_weight, preferred_element_type=jnp.float32
-    )
-    padded = jnp.zeros((adapter_count,) + partial_latent.shape[1:], jnp.float32)
-    padded = lax.dynamic_update_slice_in_dim(padded, partial_latent, grp_index * per_group, 0)
-    latent_all = lax.psum(padded, ("grp", "tp")).astype(jnp.bfloat16)
-    local_latent = lax.dynamic_slice_in_dim(
-        latent_all, tp_index * per_tensor_part, per_tensor_part, 0
+    ).astype(jnp.bfloat16)
+    packed = partial_latent.reshape(per_group * MOST * rank // 128, 128)
+    partial_all = gathered(packed, "grp", grp_size)
+    shares = exchange(partial_all.reshape(tp_size, -1, 128), "tp")
+    local_latent = (
+        jnp.sum(shares.astype(jnp.float32), axis=0)
+        .astype(jnp.bfloat16)
+        .reshape(per_tensor_part, MOST, rank)
     )
     slot_delta = jnp.einsum(
         "tsl,tlx->tsx", local_latent, adapter_up_weight, preferred_element_type=jnp.float32
@@ -96,11 +100,18 @@
     ).astype(jnp.float32)
     delta_rows = jnp.einsum("amr,amf->rf", up_select, slot_delta, precision=lax.Precision.HIGHEST)
     term_sum = jnp.dot(all_rows, output_projection, preferred_element_type=jnp.float32) + delta_rows
+    width = term_sum.shape[1]
     own_rows = residual.shape[0]
-    term_sum = term_sum + lax.dynamic_update_slice_in_dim(
-        jnp.zeros_like(term_sum), residual.astype(jnp.float32), tp_index * own_rows, 0
+    from_y = exchange(term_sum.astype(jnp.bfloat16).reshape(TP_Y, -1, width), "tp", ACROSS_Y)
+    y_sum = jnp.sum(from_y.astype(jnp.float32), axis=0)
+    from_xc = exchange(
+        y_sum.astype(jnp.bfloat16).reshape(TP_XC, own_rows, width), "tp", ACROSS_XC
     )
-    layer_out = lax.psum(term_sum, "tp").astype(jnp.bfloat16)
+    own_out = (
+        jnp.sum(from_xc.astype(jnp.float32), axis=0) + residual.astype(jnp.float32)
+    ).astype(jnp.bfloat16)
+    strip = gathered(own_out, "tp", TP_XC, ACROSS_XC).reshape(-1, width)
+    layer_out = gathered(strip, "tp", TP_Y, ACROSS_Y).reshape(row_total, width)
     layer_float = layer_out.astype(jnp.float32)
     square_part = jnp.sum(layer_float * layer_float, axis=1)
     scaled = (layer_float * final_norm_gain.astype(jnp.float32)[None, :]).astype(jnp.bfloat16)
@@ -110,12 +121,14 @@
         lax.psum_scatter(square_part, "grp", scatter_dimension=0, tiled=True),
     )
     factor = lax.rsqrt(squares / MODEL_WIDTH + EPSILON)
+    own_count = logit_rows.shape[0]
+    states = lax.dynamic_slice_in_dim(row_grammar_state, grp_index * own_count, own_count, 0)
+    allowed = lax.optimization_barrier(row_masks(unpack_bits(grammar_token_bits), states))
     logits = logit_rows * factor[:, None]
-    own_count = logits.shape[0]
-    states = lax.dynamic_slice_in_dim(row_grammar_state, grp_index * own_count, own_count, 0)
-    allowed = row_masks(unpack_bits(grammar_token_bits), states)
-    highest, summed = softmax_parts(logits, allowed)
-    highest, summed = combined_all((highest, summed), "tp", combine_stats)
+    stats = jnp.stack(softmax_parts(logits, allowed))
+    everyone = gathered(stats, "tp", tp_size)
+    highest = jnp.max(everyone[:, 0], axis=0)
+    summed = jnp.sum(everyone[:, 1] * jnp.exp(everyone[:, 0] - highest[None]), axis=0)
     return jnp.where(allowed, logits - highest[:, None] - jnp.log(summed)[:, None], 0.0)
 
 

time: 450 us -> 226 us (0.50)
  blocking collectives: 370 us -> 100 us
  starting transfers between devices: 0.01 us -> 30.3 us
  waiting for transfers between devices: 36.9 us -> 56.9 us
    psum x2 -> x0, blocking collectives: 244 us -> none  [the longest x1 133 us: body(): layer_out = lax.psum(term_sum, 'tp').astype(jnp.bfloat16)]
    all_to_all x0 -> x5, blocking collectives: none -> 75.7 us  [exchange(): lax.all_to_all(blocks, axis, 0, 0, tiled=True, axis_index_groups=groups)]
    unnamed x2 -> x1, blocking collectives: 96.2 us -> 24.5 us
    all_gather x1 -> x0, blocking collectives: 30.6 us -> none  [body(): all_rows = lax.all_gather(attention_output, 'grp', axis=0, tiled=True)]
    all_to_all x0 -> x3, starting transfers between devices: none -> 30.2 us  [exchange(): lax.all_to_all(blocks, axis, 0, 0, tiled=True, axis_index_groups=groups)]
    all_to_all x0 -> x3, waiting for transfers between devices: none -> 28 us  [exchange(): lax.all_to_all(blocks, axis, 0, 0, tiled=True, axis_index_groups=groups)]
    reduce_scatter x1, waiting for transfers between devices: 36.9 us -> 28.9 us  [body(): lax.psum_scatter(logit_part, 'grp', scatter_dimension=0, tiled=True)]
  transfers between devices with their start and end apart: 1 -> 4, of which waited for: 1 -> 4; matrix products, arithmetic and copies ran while one was open for 1% -> 4% of each run, Pallas kernels for 0% -> 0%
where the time goes in v1:
time: 226 us; the launch traced here: 225 us
  blocking collectives  100 us (44%)
  waiting for transfers between devices  56.9 us (25%)
  starting transfers between devices  30.3 us (13%)
  between operations  14.3 us (6%)
  local copies, waits for them, and re-layouts  8.25 us (4%)
  matrix products  8.12 us (4%)
  other arithmetic  6.57 us (3%)
    all_to_all x5, blocking collectives, exchange(): lax.all_to_all(blocks, axis, 0, 0, tiled=True, axis_index_groups=groups)  75.7 us
    all_to_all x3, starting transfers between devices, exchange(): lax.all_to_all(blocks, axis, 0, 0, tiled=True, axis_index_groups=groups)  30.2 us
    reduce_scatter x1, waiting for transfers between devices, body(): lax.psum_scatter(logit_part, 'grp', scatter_dimension=0, tiled=True)  28.9 us
    all_to_all x3, waiting for transfers between devices, exchange(): lax.all_to_all(blocks, axis, 0, 0, tiled=True, axis_index_groups=groups)  28 us
    unnamed x1, blocking collectives  24.5 us
  transfers between devices with their start and end apart: 4, of which 4 were waited for; matrix products, arithmetic and copies ran while one was open for 4% of the time, Pallas kernels for 0%

profile of v1, /device:TPU:1, one launch (start us, length us, event | category | flops | bytes accessed | tf_op | source)
XLA Modules:
  0.0 224.7 jit_solution(17597969422023578622)
XLA Ops:
  6.5 1.6 broadcast_in_dim.20
  8.1 15.9 %all-to-all-start = ((bf16[16,32,256]{2,1,0:T(8,128)(2,1)}), bf16[16,32,256]{2,1,0:T(8,128)(2,1)S(1)}, u32[]{:S(2)}, u32[]{:S(2)}) async-start(bf16[16,32,256]{2,1,0:T(8,128)(2,1)} %broadcast_in_dim.20), calls=%async_computation | async-start | bytes 524288 | tf_op jit(solution)/shard_map/all_to_all | solution.py:20
  24.0 0.8 copy.27
  25.6 0.4 fusion
  26.0 11.8 %all-to-all-done = bf16[16,32,256]{2,1,0:T(8,128)(2,1)S(1)} async-done(((bf16[16,32,256]{2,1,0:T(8,128)(2,1)}), bf16[16,32,256]{2,1,0:T(8,128)(2,1)S(1)}, u32[]{:S(2)}, u32[]{:S(2)}) %all-to-all-start) | async-done | bytes 262176 | tf_op jit(solution)/shard_map/all_to_all | solution.py:20
  38.0 1.3 convolution_convert_fusion.1
  39.4 22.2 %all_to_all.40 = bf16[16,32,128]{2,1,0:T(8,128)(2,1)} all-to-all(bf16[16,32,128]{2,1,0:T(8,128)(2,1)S(1)} %broadcast_in_dim.22), channel_id=1, replica_groups=mesh['grp'=16,'tp'=32] {'grp'}, dimensions={0} | all-to-all | bytes 262144 | tf_op jit(solution)/shard_map/all_to_all | solution.py:20
  61.6 10.9 %all-to-all-start.2 = ((bf16[32,16,128]{2,1,0:T(8,128)(2,1)}), bf16[32,16,128]{2,1,0:T(8,128)(2,1)S(1)}, u32[]{:S(2)}, u32[]{:S(2)}) async-start(bf16[32,16,128]{2,1,0:T(8,128)(2,1)} %bitcast.5), calls=%async_computation.2 | async-start | bytes 262144 | tf_op jit(solution)/shard_map/all_to_all | solution.py:20
  72.5 7.6 %all-to-all-done.2 = bf16[32,16,128]{2,1,0:T(8,128)(2,1)S(1)} async-done(((bf16[32,16,128]{2,1,0:T(8,128)(2,1)}), bf16[32,16,128]{2,1,0:T(8,128)(2,1)S(1)}, u32[]{:S(2)}, u32[]{:S(2)}) %all-to-all-start.2) | async-done | bytes 131104 | tf_op jit(solution)/shard_map/all_to_all | solution.py:20
  80.2 1.2 fusion.23
  81.4 0.6 convolution_bitcast_fusion
  82.0 0.3 fusion.1
  82.4 11.6 %all_to_all.41 = bf16[4,128,512]{2,1,0:T(8,128)(2,1)S(1)} all-to-all(bf16[4,128,512]{2,1,0:T(8,128)(2,1)S(1)} %bitcast.36), channel_id=1, replica_groups={{0,8,16,24},{1,9,17,25},{2,10,18,26},{3,11,19,27},{4,12,20,28},{5,13,21..., dimensions={0} | all-to-all | bytes 1048576 | tf_op jit(solution)/shard_map/all_to_all | solution.py:20
  94.0 8.9 %all_to_all.42 = bf16[8,16,512]{2,1,0:T(8,128)(2,1)S(1)} all-to-all(bf16[8,16,512]{2,1,0:T(8,128)(2,1)S(1)} %bitcast.38), channel_id=1, replica_groups={{0,1,2,3,4,5,6,7},{8,9,10,11,12,13,14,15},{16,17,18,19,20,21,22,23},{24..., dimensions={0} | all-to-all | bytes 262144 | tf_op jit(solution)/shard_map/all_to_all | solution.py:20
  103.0 8.5 %all_to_all.43 = bf16[8,16,512]{2,1,0:T(8,128)(2,1)S(1)} all-to-all(bf16[8,16,512]{2,1,0:T(8,128)(2,1)S(1)} %broadcast_in_dim.23), channel_id=1, replica_groups={{0,1,2,3,4,5,6,7},{8,9,10,11,12,13,14,15},{16,17,18,19,20,21,22,23},{24..., dimensions={0} | all-to-all | bytes 262144 | tf_op jit(solution)/shard_map/all_to_all | solution.py:20
  111.5 0.8 broadcast_in_dim.25
  112.3 3.5 %all-to-all-start.6 = ((bf16[4,128,512]{2,1,0:T(8,128)(2,1)}), bf16[4,128,512]{2,1,0:T(8,128)(2,1)S(1)}, u32[]{:S(2)}, u32[]{:S(2)}) async-start(bf16[4,128,512]{2,1,0:T(8,128)(2,1)} %broadcast_in_dim.25), calls=%async_computation.6 | async-start | bytes 1048576 | tf_op jit(solution)/shard_map/all_to_all | solution.py:20
  115.8 8.6 %all-to-all-done.6 = bf16[4,128,512]{2,1,0:T(8,128)(2,1)S(1)} async-done(((bf16[4,128,512]{2,1,0:T(8,128)(2,1)}), bf16[4,128,512]{2,1,0:T(8,128)(2,1)S(1)}, u32[]{:S(2)}, u32[]{:S(2)}) %all-to-all-start.6) | async-done | bytes 524320 | tf_op jit(solution)/shard_map/all_to_all | solution.py:20
  124.5 3.2 %fusion.24 = f32[512,2048]{1,0:T(8,128)} fusion(bf16[512,512]{1,0:T(8,128)(2,1)S(1)} %fusion.2, bf16[512,2048]{1,0:T(8,128)(2,1)S(1)} %copy-done), kind=kOutput, calls=%fused_computation.46 | convolution fusion | flops 1073741824 | bytes 6815744 | tf_op jit(solution)/shard_map/dot_general | solution.py:118
  127.9 0.6 copy-done.3
  128.5 0.4 shift_right_arithmetic.20
  128.9 1.3 shift_right_arithmetic.21
  130.2 0.8 dynamic_slice.9
  131.0 1.3 convolution_compare_fusion
  132.3 1.3 dynamic-slice
  134.2 1.2 multiply_reduce_fusion
  135.5 24.5 %all-reduce = f32[512]{0:T(512)S(1)} all-reduce(f32[512]{0:T(512)S(1)} %bitcast.43), channel_id=3, replica_groups=mesh['grp'=16,'tp'=32] {'grp'}, use_global_device_ids=true, to_apply=%region_7.8.clone | all-reduce | flops 512 | bytes 4096
  160.1 28.9 %reduce-scatter.2.cloned.1.call-done = f32[32,2048]{1,0:T(8,128)} async-done(((f32[512,2048]{1,0:T(8,128)}), f32[32,2048]{1,0:T(8,128)}) %reduce-scatter.2.cloned.1.call-update) | async-done | bytes 262160 | tf_op jit(solution)/shard_map/reduce_scatter | solution.py:120
  189.0 1.2 fusion.9
  190.1 1.2 exponential_reduce_fusion
  191.4 24.6 %all_to_all.44 = f32[32,2,32]{2,1,0:T(2,128)S(1)} all-to-all(f32[32,2,32]{2,1,0:T(2,128)S(1)} %broadcast_in_dim.28), channel_id=1, replica_groups=mesh['grp'=16,'tp'=32] {'tp'}, dimensions={0} | all-to-all | bytes 16384 | tf_op jit(solution)/shard_map/all_to_all | solution.py:20
  216.1 1.8 subtract_select_fusion
  (43 shorter events, 1.7 us)
Async XLA Ops:
  6.5 118.0 %copy-start = (bf16[512,2048]{1,0:T(8,128)(2,1)S(1)}, bf16[512,2048]{1,0:T(8,128)(2,1)}, u32[]{:S(2)}) copy-start(bf16[512,2048]{1,0:T(8,128)(2,1)} %param.16) | copy-start | bytes 6291460
  8.1 17.4 %copy-start.5 = (s32[512]{0:T(512)S(1)}, s32[512]{0:T(512)}, u32[]{:S(2)}) copy-start(s32[512]{0:T(512)} %param.17) | copy-start | bytes 6148
  8.1 29.6 %all-to-all-start = ((bf16[16,32,256]{2,1,0:T(8,128)(2,1)}), bf16[16,32,256]{2,1,0:T(8,128)(2,1)S(1)}, u32[]{:S(2)}, u32[]{:S(2)}) async-start(bf16[16,32,256]{2,1,0:T(8,128)(2,1)} %broadcast_in_dim.20), calls=%async_computation | async-start | bytes 524288 | tf_op jit(solution)/shard_map/all_to_all | solution.py:20
  26.0 56.1 %copy-start.2 = (bf16[256,512]{1,0:T(8,128)(2,1)S(1)}, bf16[256,512]{1,0:T(8,128)(2,1)}, u32[]{:S(2)}) copy-start(bf16[256,512]{1,0:T(8,128)(2,1)} %param.11) | copy-start | bytes 786436
  61.6 18.5 %all-to-all-start.2 = ((bf16[32,16,128]{2,1,0:T(8,128)(2,1)}), bf16[32,16,128]{2,1,0:T(8,128)(2,1)S(1)}, u32[]{:S(2)}, u32[]{:S(2)}) async-start(bf16[32,16,128]{2,1,0:T(8,128)(2,1)} %bitcast.5), calls=%async_computation.2 | async-start | bytes 262144 | tf_op jit(solution)/shard_map/all_to_all | solution.py:20
  82.0 20.9 %copy-start.4 = (bf16[16,512]{1,0:T(8,128)(2,1)S(1)}, bf16[16,512]{1,0:T(8,128)(2,1)}, u32[]{:S(2)}) copy-start(bf16[16,512]{1,0:T(8,128)(2,1)} %param.14) | copy-start | bytes 49156
  82.3 33.5 %copy-start.6 = (bf16[512]{0:T(512)(128)(2,1)S(1)}, bf16[512]{0:T(512)(128)(2,1)}, u32[]{:S(2)}) copy-start(bf16[512]{0:T(512)(128)(2,1)} %param.15) | copy-start | bytes 3076
  112.3 12.2 %all-to-all-start.6 = ((bf16[4,128,512]{2,1,0:T(8,128)(2,1)}), bf16[4,128,512]{2,1,0:T(8,128)(2,1)S(1)}, u32[]{:S(2)}, u32[]{:S(2)}) async-start(bf16[4,128,512]{2,1,0:T(8,128)(2,1)} %broadcast_in_dim.25), calls=%async_computation.6 | async-start | bytes 1048576 | tf_op jit(solution)/shard_map/all_to_all | solution.py:20
  115.8 73.2 %reduce-scatter.2.cloned.1.call-start = ((), (), s32[]{:S(2)}) async-start(), calls=%async_computation.9 | async-start | bytes 4456448 | tf_op jit(solution)/shard_map/reduce_scatter | solution.py:120
  124.4 3.3 %copy-start.1 = (bf16[4,128,512]{2,1,0:T(8,128)(2,1)}, bf16[4,128,512]{2,1,0:T(8,128)(2,1)S(1)}, u32[]{:S(2)}) copy-start(bf16[4,128,512]{2,1,0:T(8,128)(2,1)S(1)} %all-to-all-done.6) | copy-start | bytes 1572868
  127.8 0.7 copy-start.3
Sparse Core Ops, SparseCore 0:
  127.9 61.0 reduce-scatter.1
